TPU v7x, 256 devices: a whole 4x4x8 slice. The times are simulated.
256 devices in a mesh: gx: 64 (over x, z, core), gy: 4 (over y).
Axes of the slice: x: 4, y: 4, z: 8, core: 2. Of those that a mesh axis runs over, the one named last changes fastest.
Arguments:
- amplitudes: float32 [2, 512, 128, 512], P(None, 'gx', None, 'gy'), may hold values from -6 to 6
- integrals: float32 [2, 32, 128, 128, 512], P(None, 'gy', None, 'gx'), may hold values from -0.09375 to 0.09375
- virt_count: int32 [8], replicated, may hold values from 24 to 128, as said below
- pair_irrep: int32 [8], replicated, may hold values from 0 to 7, as said below
- slab_index: int32 [1], replicated, may hold values from 0 to 15
- occ_energy: float32 [64], replicated, may hold values from -2 to -0.3
- virt_energy: float32 [512], replicated, may hold values from 0.1 to 3
Outputs:
- update: float32 [2, 512, 32, 128], P(None, 'gx', 'gy')
Inputs may be any that keep to these rules, and one draw needn't show every extreme that they name: `virt_count`: entry k counts the virtual orbitals of irrep k; they sum to 512 and the largest is exactly 128. `pair_irrep`: a permutation of the irreps.
All inputs are finite; a program needn't handle non-finite values.
Results may differ from a plain program's by a relative error of at most 0.0001.
Values sent between devices are 32-bit elements; how exact they have to be, the bound alone decides.
No kernel may reach another device: no remote copies, remote signals or barrier semaphores. Data moves between devices by JAX's collectives and lax.ppermute only.
A program may use at most 64 MiB of HBM per device.

v0:
```python
import jax
import jax.numpy as jnp
from jax import lax
from jax.sharding import PartitionSpec as P

OCC = 64
VIRT = 512
SLAB = 32
IRREPS = 8
SYMS = 2
MAXIRR = 128


def irrep_of(positions, starts):
    return jnp.sum((positions[..., None] >= starts[1:]).astype(jnp.int32), axis=-1)


def lookup(entries, positions):
    picks = (positions[..., None] == jnp.arange(IRREPS, dtype=jnp.int32)).astype(entries.dtype)
    return jnp.sum(entries * picks, axis=-1)


def denominator_update(
    ladder, pair_rows, slab_rows, symmetry, slab_first, starts, virt_count, occ_energy, virt_energy
):
    per_irrep = OCC // IRREPS
    occ_irrep = pair_rows // (per_irrep * per_irrep)
    first_occ = per_irrep * occ_irrep + pair_rows % (per_irrep * per_irrep) // per_irrep
    second_occ = per_irrep * jnp.bitwise_xor(occ_irrep, symmetry) + pair_rows % per_irrep
    occ_sum = jnp.take(occ_energy, first_occ) + jnp.take(occ_energy, second_occ)
    slab_virt = SLAB * slab_first + slab_rows
    partner = jnp.bitwise_xor(irrep_of(slab_virt, starts), symmetry)
    block_start = lookup(starts, partner)
    block_count = lookup(virt_count, partner)
    slot_range = jnp.arange(MAXIRR, dtype=jnp.int32)
    partner_orbital = jnp.clip(block_start[:, None] + slot_range[None, :], 0, VIRT - 1)
    slot_valid = slot_range[None, :] < block_count[:, None]
    denominator = (
        occ_sum[:, None, None]
        - jnp.take(virt_energy, slab_virt)[None, :, None]
        - jnp.take(virt_energy, partner_orbital)[None]
    )
    return jnp.where(slot_valid[None], ladder / denominator, jnp.zeros_like(ladder))


def on_device(amplitudes, integrals, virt_count, pair_irrep, slab_index, occ_energy, virt_energy):
    starts = jnp.cumsum(virt_count) - virt_count
    handled = pair_irrep[:SYMS]
    pair_block = lax.axis_index("gx")
    virt_block = lax.axis_index("gy")
    slot_width = integrals.shape[3]
    slot_ids = pair_block * slot_width + jnp.arange(slot_width, dtype=jnp.int32)
    gathered = lax.all_gather(amplitudes, "gy", axis=3, tiled=True)
    spread = lax.all_to_all(gathered, "gx", split_axis=2, concat_axis=1, tiled=True)
    width = spread.shape[3]
    virt_ids = jnp.arange(width, dtype=jnp.int32)
    partner = jnp.bitwise_xor(irrep_of(virt_ids, starts)[None, :], handled[:, None])
    valid = slot_ids[None, :, None] < lookup(virt_count, partner)[:, None, :]
    masked = jnp.where(valid[:, None], spread, jnp.zeros_like(spread))
    ladder = lax.dot_general(
        masked,
        integrals,
        (((2, 3), (3, 4)), ((0,), (0,))),
        precision=lax.Precision.HIGHEST,
        preferred_element_type=jnp.float32,
    )
    by_slot = lax.psum_scatter(ladder, "gx", scatter_dimension=3, tiled=True)
    reduced = lax.all_to_all(by_slot, "gx", split_axis=1, concat_axis=3, tiled=True)
    pair_rows = pair_block * reduced.shape[1] + jnp.arange(reduced.shape[1], dtype=jnp.int32)
    slab_rows = virt_block * reduced.shape[2] + jnp.arange(reduced.shape[2], dtype=jnp.int32)
    updates = []
    for member in range(SYMS):
        updates.append(
            denominator_update(
                reduced[member],
                pair_rows,
                slab_rows,
                handled[member],
                slab_index[0],
                starts,
                virt_count,
                occ_energy,
                virt_energy,
            )
        )
    return jnp.stack(updates)


def solution(mesh):
    placed = (P(None, "gx", None, "gy"), P(None, "gy", None, "gx", None), P(), P(), P(), P(), P())
    return jax.shard_map(
        on_device, mesh=mesh, in_specs=placed, out_specs=P(None, "gx", "gy", None), check_vma=False
    )
```

profile of v0, /device:TPU:1, one launch (start us, length us, event | category | flops | bytes accessed | tf_op | source)
XLA Modules:
  0.0 371.2 jit_solution(7651302949181767710)
XLA Ops:
  6.5 2.8 copy.50
  9.4 56.5 %all-gather.2.cloned.1.call-done = f32[2,8,128,512]{3,1,0,2:T(8,128)} async-done(((f32[2,8,128,128]{3,1,0,2:T(8,128)}), f32[2,8,128,512]{3,1,0,2:T(8,128)}) %all-gather.2.cloned.1.call-update) | async-done | bytes 4194320 | tf_op jit(solution)/shard_map/all_gather | solution.py:53
  65.9 12.2 %all-to-all-start = ((f32[2,8,128,512]{3,1,0,2:T(8,128)}), f32[2,8,128,512]{3,1,0,2:T(8,128)}, u32[]{:S(2)}, u32[]{:S(2)}) async-start(f32[2,8,128,512]{3,1,0,2:T(8,128)} %all-gather.2.cloned.1.call-done), calls=%async_computation | async-start | bytes 8388608 | tf_op jit(solution)/shard_map/all_to_all | solution.py:54
  78.8 95.2 %all-to-all-done = f32[2,8,128,512]{3,1,0,2:T(8,128)} async-done(((f32[2,8,128,512]{3,1,0,2:T(8,128)}), f32[2,8,128,512]{3,1,0,2:T(8,128)}, u32[]{:S(2)}, u32[]{:S(2)}) %all-to-all-start) | async-done | bytes 4194336 | tf_op jit(solution)/shard_map/all_to_all | solution.py:54
  174.0 22.2 %fusion.4 = f32[2,512,8,128]{1,2,0,3:T(8,128)} fusion(f32[2,8,128,2,512]{4,3,2,1,0:T(2,128)} %param.14, f32[2,64,8,2,512]{4,2,0,3,1:T(8,128)} %bitcast.6, pred[2,2,512]{2,1,0:T(4,128)(4,1)S(1)} %broadcast_compare_fusion), kind=kOutput, calls=%fused_computation.11 | convolution fusion | flops 12885950464 | bytes 16779264 | tf_op jit(solution)/shard_map/dot_general | solution.py:60
  196.9 0.6 fusion.22
  197.6 1.2 broadcast_xor_fusion.1
  199.2 6.9 %gather_fusion.5 = f32[1024]{0:T(1024)S(1)} fusion(f32[512]{0:T(512)S(1)} %copy-done, s32[1024]{0:T(1024)S(1)} %bitcast_clamp_fusion), kind=kCustom, calls=%fused_computation.5.clone | custom fusion | bytes 12288 | tf_op jit(solution)/shard_map/jit(_take)/gather | solution.py:41
  206.2 0.6 gather_fusion.2
  206.9 0.6 compare_select_fusion.4
  207.5 0.6 gather_fusion.1
  208.1 0.6 gather_fusion
  208.8 0.6 gather_fusion.4
  209.5 6.9 %gather_fusion.3 = f32[1024]{0:T(1024)S(1)} fusion(f32[512]{0:T(512)S(1)} %copy-done, s32[1024]{0:T(1024)S(1)} %bitcast_clamp_fusion.1), kind=kCustom, calls=%fused_computation.2.clone | custom fusion | bytes 12288 | tf_op jit(solution)/shard_map/jit(_take)/gather | solution.py:41
  216.6 115.0 %reduce-scatter.2.cloned.1.call-done = f32[2,512,8,2]{1,2,0,3:T(8,128)} async-done(((f32[2,512,8,128]{1,2,0,3:T(8,128)}), f32[2,512,8,2]{1,2,0,3:T(8,128)}) %reduce-scatter.2.cloned.1.call-update) | async-done | bytes 65552 | tf_op jit(solution)/shard_map/reduce_scatter | solution.py:67
  331.7 1.4 copy.54
  333.1 2.2 reshape.303
  335.3 12.9 %all-to-all-start.1 = ((f32[64,1,256]{2,1,0:T(1,128)}), f32[64,1,256]{2,1,0:T(1,128)S(1)}, u32[]{:S(2)}, u32[]{:S(2)}) async-start(f32[64,1,256]{2,1,0:T(1,128)} %reshape.303), calls=%async_computation.2 | async-start | bytes 131072 | tf_op jit(solution)/shard_map/all_to_all | solution.py:68
  348.3 9.7 %all-to-all-done.1 = f32[64,1,256]{2,1,0:T(1,128)S(1)} async-done(((f32[64,1,256]{2,1,0:T(1,128)}), f32[64,1,256]{2,1,0:T(1,128)S(1)}, u32[]{:S(2)}, u32[]{:S(2)}) %all-to-all-start.1) | async-done | bytes 65568 | tf_op jit(solution)/shard_map/all_to_all | solution.py:68
  358.0 0.5 broadcast.388
  358.5 0.8 reduce
  359.3 1.6 reshape.304
  360.9 1.3 copy.66
  363.7 0.7 pad_maximum_fusion
  (45 shorter events, 3.2 us)
Async XLA Ops:
  6.5 192.6 %copy-start = (f32[512]{0:T(512)S(1)}, f32[512]{0:T(512)}, u32[]{:S(2)}) copy-start(f32[512]{0:T(512)} %param.19) | copy-start | bytes 6148
  6.5 59.4 %all-gather.2.cloned.1.call-start = ((), (), s32[]{:S(2)}) async-start(), calls=%async_computation.3 | async-start | bytes 5242880 | tf_op jit(solution)/shard_map/all_gather | solution.py:53
  9.4 68.8 %copy-start.3 = (s32[8]{0:T(128)S(1)}, s32[8]{0:T(128)}, u32[]{:S(2)}) copy-start(s32[8]{0:T(128)} %param.15) | copy-start | bytes 100
  9.4 69.2 %copy-start.2 = (s32[8]{0:T(128)S(1)}, s32[8]{0:T(128)}, u32[]{:S(2)}) copy-start(s32[8]{0:T(128)} %param.16) | copy-start | bytes 100
  65.9 108.1 %all-to-all-start = ((f32[2,8,128,512]{3,1,0,2:T(8,128)}), f32[2,8,128,512]{3,1,0,2:T(8,128)}, u32[]{:S(2)}, u32[]{:S(2)}) async-start(f32[2,8,128,512]{3,1,0,2:T(8,128)} %all-gather.2.cloned.1.call-done), calls=%async_computation | async-start | bytes 8388608 | tf_op jit(solution)/shard_map/all_to_all | solution.py:54
  78.1 253.5 %reduce-scatter.2.cloned.1.call-start = ((), (), s32[]{:S(2)}) async-start(), calls=%async_computation.4 | async-start | bytes 4259840 | tf_op jit(solution)/shard_map/reduce_scatter | solution.py:67
  196.2 11.3 %copy-start.1 = (f32[64]{0:T(128)S(1)}, f32[64]{0:T(128)}, u32[]{:S(2)}) copy-start(f32[64]{0:T(128)} %param.18) | copy-start | bytes 772
  335.3 22.7 %all-to-all-start.1 = ((f32[64,1,256]{2,1,0:T(1,128)}), f32[64,1,256]{2,1,0:T(1,128)S(1)}, u32[]{:S(2)}, u32[]{:S(2)}) async-start(f32[64,1,256]{2,1,0:T(1,128)} %reshape.303), calls=%async_computation.2 | async-start | bytes 131072 | tf_op jit(solution)/shard_map/all_to_all | solution.py:68
Sparse Core Ops, SparseCore 0:
  9.5 56.3 all-gather.1
  196.3 135.2 reduce-scatter.1
where the time goes:
time: 372 us; the launch traced here: 371 us
  waiting for transfers between devices  276 us (74%)
  local copies, waits for them, and re-layouts  28.2 us (8%)
  starting transfers between devices  25.2 us (7%)
  matrix products  22.2 us (6%)
  between operations  14.3 us (4%)
  other arithmetic  4.9 us (1%)
    reduce_scatter x1, waiting for transfers between devices, on_device(): by_slot = lax.psum_scatter(ladder, 'gx', scatter_dimension=3, tiled=True)  115 us
    all_to_all x1, waiting for transfers between devices, on_device(): lax.all_to_all(gathered, 'gx', split_axis=2, concat_axis=1, tiled=True)  95.2 us
    all_gather x1, waiting for transfers between devices, on_device(): gathered = lax.all_gather(amplitudes, 'gy', axis=3, tiled=True)  56.5 us
    dot_general x1, matrix products, on_device(): lax.dot_general(masked, integrals, (((2, 3), (3, 4)), ((0,), (0,))), prec...  22.2 us
    gather x2, local copies, waits for them, and re-layouts, denominator_update(): jnp.take(virt_energy, partner_orbital)[None]  13.7 us
    all_to_all x1, starting transfers between devices, on_device(): lax.all_to_all(by_slot, 'gx', split_axis=1, concat_axis=3, tiled=True)  12.9 us
    all_to_all x1, starting transfers between devices, on_device(): lax.all_to_all(gathered, 'gx', split_axis=2, concat_axis=1, tiled=True)  12.2 us
    all_to_all x1, waiting for transfers between devices, on_device(): lax.all_to_all(by_slot, 'gx', split_axis=1, concat_axis=3, tiled=True)  9.7 us
  transfers between devices with their start and end apart: 4, of which 4 were waited for; matrix products, arithmetic and copies ran while one was open for 5% of the time, Pallas kernels for 0%

commit v1 on v0

v1 whole, which is shorter than its diff:
```python
import jax
import jax.numpy as jnp
from jax import lax
from jax.sharding import Mesh
from jax.sharding import PartitionSpec as P

OCC = 64
VIRT = 512
SLAB = 32
IRREPS = 8
SYMS = 2
MAXIRR = 128
GX = ("x", "z", "c")


def irrep_of(positions, starts):
    return jnp.sum((positions[..., None] >= starts[1:]).astype(jnp.int32), axis=-1)


def lookup(entries, positions):
    picks = positions[..., None] == jnp.arange(IRREPS, dtype=jnp.int32)
    return jnp.sum(jnp.where(picks, entries, jnp.zeros_like(entries)), axis=-1)


def take(table, positions):
    picks = positions[..., None] == jnp.arange(table.shape[0], dtype=jnp.int32)
    return jnp.sum(jnp.where(picks, table, jnp.zeros_like(table)), axis=-1)


def denominators(pair_rows, slab_rows, symmetry, slab_first, starts, virt_count, occ, virt):
    per = OCC // IRREPS
    occ_irrep = pair_rows // (per * per)
    first = per * occ_irrep + pair_rows % (per * per) // per
    second = per * jnp.bitwise_xor(occ_irrep, symmetry) + pair_rows % per
    occ_sum = take(occ, first) + take(occ, second)
    slab_virt = SLAB * slab_first + slab_rows
    partner = jnp.bitwise_xor(irrep_of(slab_virt, starts), symmetry)
    slots = jnp.arange(MAXIRR, dtype=jnp.int32)
    orbital = jnp.clip(lookup(starts, partner)[:, None] + slots[None, :], 0, VIRT - 1)
    valid = slots[None, :] < lookup(virt_count, partner)[:, None]
    denominator = occ_sum[:, None, None] - take(virt, slab_virt)[None, :, None] - take(virt, orbital)[None]
    return denominator, jnp.broadcast_to(valid[None], denominator.shape)


def shift(value, axis, size, by):
    return lax.ppermute(value, axis, [(i, (i + by) % size) for i in range(size)])


def on_device(amplitudes, integrals, virt_count, pair_irrep, slab_index, occ_energy, virt_energy):
    starts = jnp.cumsum(virt_count) - virt_count
    handled = pair_irrep[:SYMS]
    core = lax.axis_index("c")
    y = lax.axis_index("y")
    chip = lax.axis_index("x") * 8 + lax.axis_index("z")
    block = chip * 2 + core

    send = amplitudes.reshape(2, 8, 32, 4, 128).transpose(2, 0, 3, 1, 4).reshape(64, 4, 8, 128)
    spread = lax.all_to_all(send, GX, split_axis=0, concat_axis=0, tiled=True)

    other = shift(lax.dynamic_index_in_dim(integrals, 1 - core, 0, False), "c", 2, 1)
    own = lax.dynamic_index_in_dim(integrals, core, 0, False)
    first = core == 0
    low = jnp.where(first, own, other)
    high = jnp.where(first, other, own)
    pieces = jnp.concatenate([low, high], axis=2)
    virt_ids = jnp.arange(VIRT, dtype=jnp.int32)
    partner = jnp.bitwise_xor(irrep_of(virt_ids, starts), handled[core])
    slot_ids = 4 * chip + jnp.arange(4, dtype=jnp.int32)
    valid = slot_ids[:, None] < lookup(virt_count, partner)[None, :]
    pieces = jnp.where(valid[None, None], pieces, jnp.zeros_like(pieces))

    up = shift(spread, "y", 4, 1)
    down = shift(spread, "y", 4, -1)
    half = 32
    far = jnp.concatenate([shift(up[:half], "y", 4, 1), shift(down[half:], "y", 4, -1)], axis=0)
    ladder = 0.0
    for hop, part in ((0, spread), (1, up), (-1, down), (2, far)):
        quarter = lax.dynamic_slice_in_dim(pieces, 128 * ((y - hop) % 4), 128, 3)
        ladder = ladder + lax.dot_general(
            part,
            quarter,
            (((1, 3), (2, 3)), ((), ())),
            precision=lax.Precision.HIGH,
            preferred_element_type=jnp.float32,
        )
    sums = lax.all_to_all(ladder.reshape(4, 16, 8, 8, 128), "x", 0, 0, tiled=True).sum(0)
    sums = lax.all_to_all(sums, ("z", "c"), 0, 0, tiled=True)
    sums = sums.reshape(8, 2, 8, 8, 128).sum(0)

    pair_rows = block * 8 + jnp.arange(8, dtype=jnp.int32)
    slab_rows = y * 8 + jnp.arange(8, dtype=jnp.int32)
    updates = []
    for member in range(SYMS):
        denominator, keep = denominators(
            pair_rows, slab_rows, handled[member], slab_index[0], starts, virt_count, occ_energy, virt_energy
        )
        updates.append(jnp.where(keep, sums[member] / denominator, jnp.zeros_like(denominator)))
    return jnp.stack(updates)


def solution(mesh):
    fine = Mesh(mesh.devices.reshape(4, 8, 2, 4), ("x", "z", "c", "y"))
    placed = (P(None, GX, None, "y"), P(None, "y", None, GX, None), P(), P(), P(), P(), P())
    return jax.shard_map(
        on_device, mesh=fine, in_specs=placed, out_specs=P(None, GX, "y", None), check_vma=False
    )
```

time: 372 us -> 165 us (0.44)
  waiting for transfers between devices: 276 us -> 58 us
  blocking collectives: 0 us -> 38.2 us
  between operations: 14.3 us -> 0.86 us
  other arithmetic: 4.9 us -> 16.5 us
  matrix products: 22.2 us -> 11.8 us
  local copies, waits for them, and re-layouts: 28.2 us -> 20.2 us
  starting transfers between devices: 25.2 us -> 18.8 us
    reduce_scatter x1 -> x0, waiting for transfers between devices: 115 us -> none  [on_device(): by_slot = lax.psum_scatter(ladder, 'gx', scatter_dimension=3, tiled=True)]
    all_to_all x2, waiting for transfers between devices: 105 us -> 36.3 us  [the longest x1 20.4 us: on_device(): lax.all_to_all(ladder.reshape(4, 16, 8, 8, 128), 'x', 0, 0, tiled=True)]
    all_gather x1 -> x0, waiting for transfers between devices: 56.5 us -> none  [on_device(): gathered = lax.all_gather(amplitudes, 'gy', axis=3, tiled=True)]
    all_to_all x0 -> x1, blocking collectives: none -> 38.2 us  [on_device(): spread = lax.all_to_all(send, GX, split_axis=0, concat_axis=0, tiled=True)]
    ppermute x0 -> x5, waiting for transfers between devices: none -> 21.7 us  [shift(): lax.ppermute(value, axis, [(i, (i + by) % size) for i in range(size)])]
    gather x6 -> x0, local copies, waits for them, and re-layouts: 16.3 us -> none  [the longest x2 13.7 us: denominator_update(): jnp.take(virt_energy, partner_orbital)[None]]
    all_to_all x2, starting transfers between devices: 25.1 us -> 10.2 us  [the longest x1 6.46 us: on_device(): sums = lax.all_to_all(sums, ('z', 'c'), 0, 0, tiled=True)]
    dynamic_slice x0 -> x3, local copies, waits for them, and re-layouts: none -> 11.6 us  [the longest x1 8.27 us: on_device(): own = lax.dynamic_index_in_dim(integrals, core, 0, False)]
  transfers between devices with their start and end apart: 4 -> 7, of which waited for: 4 -> 3; matrix products, arithmetic and copies ran while one was open for 5% -> 18% of each run, Pallas kernels for 0% -> 0%
where the time goes in v1:
time: 165 us; the launch traced here: 164 us
  waiting for transfers between devices  58 us (35%)
  blocking collectives  38.2 us (23%)
  local copies, waits for them, and re-layouts  20.2 us (12%)
  starting transfers between devices  18.8 us (11%)
  other arithmetic  16.5 us (10%)
  matrix products  11.8 us (7%)
    all_to_all x1, blocking collectives, on_device(): spread = lax.all_to_all(send, GX, split_axis=0, concat_axis=0, tiled=True)  38.2 us
    ppermute x5, waiting for transfers between devices, shift(): lax.ppermute(value, axis, [(i, (i + by) % size) for i in range(size)])  21.7 us
    all_to_all x1, waiting for transfers between devices, on_device(): lax.all_to_all(ladder.reshape(4, 16, 8, 8, 128), 'x', 0, 0, tiled=True)  20.4 us
    all_to_all x1, waiting for transfers between devices, on_device(): sums = lax.all_to_all(sums, ('z', 'c'), 0, 0, tiled=True)  15.9 us
    dot_general x4, matrix products, on_device(): lax.dot_general(part, quarter, (((1, 3), (2, 3)), ((), ())), precision=la...  11.8 us
    ppermute x5, starting transfers between devices, shift(): lax.ppermute(value, axis, [(i, (i + by) % size) for i in range(size)])  8.61 us
    dynamic_slice x1, local copies, waits for them, and re-layouts, on_device(): own = lax.dynamic_index_in_dim(integrals, core, 0, False)  8.27 us
    select_n x1, other arithmetic, on_device(): low = jnp.where(first, own, other)  6.96 us
  transfers between devices with their start and end apart: 7, of which 3 were waited for; matrix products, arithmetic and copies ran while one was open for 18% of the time, Pallas kernels for 0%

profile of v1, /device:TPU:1, one launch (start us, length us, event | category | flops | bytes accessed | tf_op | source)
XLA Modules:
  0.0 164.4 jit_solution(11105643393446316410)
XLA Ops:
  0.0 8.3 %constant_dynamic-slice_fusion.1 = (f32[1,8,128,2,512]{4,3,2,1,0:T(2,128)}, f32[1,8,128,2,512]{4,3,2,1,0:T(2,128)S(1)}) fusion(f32[2,8,128,2,512]{4,3,2,1,0:T(2,128)} %param.8, s32[]{:T(128)S(6)} %select_n.154, s32[]{:T(128)S(6)} %select_n.157), kind=kLoop, calls=%fused_computation.69 | loop fusion | bytes 16777224 | tf_op jit(solution)/shard_map/jit(dynamic_index_in_dim)/dynamic_slice | solution.py:61
  8.3 2.8 %copy.71 = f32[1,8,128,2,512]{4,2,3,1,0:T(8,128)} copy(f32[1,8,128,2,512]{4,3,2,1,0:T(2,128)S(1)} %get-tuple-element.17) | data formatting | bytes 8388608 | tf_op jit(solution)/shard_map/jit(dynamic_index_in_dim)/dynamic_slice | solution.py:60
  11.0 3.2 %collective-permute-start = (f32[8,128,2,512]{3,1,2,0:T(8,128)}, f32[8,128,2,512]{3,1,2,0:T(8,128)}, u32[]{:S(2)}, u32[]{:S(2)}) collective-permute-start(f32[8,128,2,512]{3,1,2,0:T(8,128)} %bitcast.71), channel_id=1, source_target_pairs={{0,4},{4,0},{1,5},{5,1},{2,6},{6,2},{3,7},{7,3},{8,12},{12,8},{9,1... | collective-permute-start | bytes 12582920 | tf_op jit(solution)/shard_map/ppermute | solution.py:46
  14.5 38.2 %all_to_all.15 = f32[64,4,8,128]{3,1,2,0:T(4,128)S(1)} all-to-all(f32[64,4,8,128]{3,1,2,0:T(4,128)S(1)} %bitcast.74), channel_id=1, replica_groups=mesh['x'=4,'z'=8,'c'=2,'y'=4] {'x','z','c'}, dimensions={0} | all-to-all | bytes 2097152 | tf_op jit(solution)/shard_map/all_to_all | solution.py:58
  52.8 1.6 copy.39
  54.4 1.3 collective-permute-start.1
  55.6 1.4 collective-permute-start.2
  58.8 21.7 %collective-permute-done.1 = f32[64,4,8,128]{3,0,1,2:T(8,128)S(1)} collective-permute-done((f32[64,4,8,128]{3,0,1,2:T(8,128)}, f32[64,4,8,128]{3,0,1,2:T(8,128)S(1)}, u32[]{:S(2)}, u32[]{:S(2)}) %collective-permute-start.1) | collective-permute-done | bytes 1048608 | tf_op jit(solution)/shard_map/ppermute | solution.py:46
  81.5 1.9 %slice.37 = f32[32,4,8,128]{3,0,1,2:T(8,128)} slice(f32[64,4,8,128]{3,0,1,2:T(8,128)} %collective-permute-done.2), slice={[32:64], [0:4], [0:8], [0:128]} | slice | bytes 1048576 | tf_op jit(solution)/shard_map/slice | solution.py:75
  83.4 2.6 %collective-permute-start.4 = (f32[32,4,8,128]{3,0,1,2:T(8,128)}, f32[32,4,8,128]{3,0,1,2:T(8,128)}, u32[]{:S(2)}, u32[]{:S(2)}) collective-permute-start(f32[32,4,8,128]{3,0,1,2:T(8,128)} %slice.37), channel_id=1, source_target_pairs={{0,3},{1,0},{2,1},{3,2},{4,7},{5,4},{6,5},{7,6},{8,11},{9,8},{10,9... | collective-permute-start | bytes 1572872 | tf_op jit(solution)/shard_map/ppermute | solution.py:46
  86.0 7.0 %bitcast_select_fusion.1 = (f32[8,128,2,512]{3,1,2,0:T(8,128)S(1)}, f32[8,128,2,512]{3,1,2,0:T(8,128)}) fusion(f32[8,128,2,512]{3,1,2,0:T(8,128)} %collective-permute-done, f32[1,8,128,2,512]{4,3,2,1,0:T(2,128)} %get-tuple-element.16, pred[]{:T(512)S(6)} %eq.72), kind=kLoop, calls=%fused_computation.2 | loop fusion | flops 2097152 | bytes 16777216 | tf_op jit(solution)/shard_map/jit(_where)/select_n | solution.py:63
  93.0 3.4 %maximum_select_fusion = f32[8,128,4,512]{3,1,2,0:T(8,128)S(1)} fusion(f32[8,128,2,512]{3,1,2,0:T(8,128)} %get-tuple-element.15, f32[8,128,2,512]{3,1,2,0:T(8,128)S(1)} %get-tuple-element.14, pred[4,512]{1,0:T(4,128)(4,1)S(1)} %broadcast_compare_fusion), kind=kLoop, calls=%fused_computation | loop fusion | flops 4194304 | bytes 16779264 | tf_op jit(solution)/shard_map/jit(_where)/select_n | solution.py:70
  96.4 3.1 %fusion.4 = f32[8,128,64,8,1]{1,2,4,3,0:T(8,128)S(1)} fusion(f32[8,128,4,512]{3,1,2,0:T(8,128)S(1)} %maximum_select_fusion, s32[]{:T(128)S(6)} %select_n.164, f32[64,4,8,128]{3,0,1,2:T(8,128)} %copy-done), kind=kOutput, calls=%fused_computation.8 | convolution fusion | flops 1610612736 | bytes 5242884 | tf_op jit(solution)/shard_map/dot_general | solution.py:79
  99.5 3.1 %fusion.2 = f32[8,128,64,8,1]{1,2,4,3,0:T(8,128)S(1)} fusion(f32[8,128,4,512]{3,1,2,0:T(8,128)S(1)} %maximum_select_fusion, s32[]{:T(128)S(6)} %select_n.166, f32[64,4,8,128]{3,0,1,2:T(8,128)} %collective-permute-done.2), kind=kOutput, calls=%fused_computation.6 | convolution fusion | flops 1610612736 | bytes 5242884 | tf_op jit(solution)/shard_map/dot_general | solution.py:79
  102.6 2.3 %fusion.6 = f32[8,128,64,8,1]{1,2,4,3,0:T(8,128)S(1)} fusion(f32[8,128,4,512]{3,1,2,0:T(8,128)S(1)} %maximum_select_fusion, s32[]{:T(128)S(6)} %select_n.162, f32[64,4,8,128]{3,1,2,0:T(4,128)S(1)} %all_to_all.15), kind=kOutput, calls=%fused_computation.10 | convolution fusion | flops 1610612736 | bytes 5242884 | tf_op jit(solution)/shard_map/dot_general | solution.py:79
  105.0 3.3 %bitcast_add_fusion = f32[64,8,8,128]{3,0,1,2:T(8,128)S(1)} fusion(f32[8,128,64,8,1]{1,2,4,3,0:T(8,128)S(1)} %fusion.2, f32[8,128,64,8,1]{1,2,4,3,0:T(8,128)S(1)} %fusion.4, f32[8,128,64,8,1]{1,2,4,3,0:T(8,128)S(1)} %fusion.6, f32[8,128,4,512]{3,1,2,0:T(8,128)S(1)} %maximum_select_fusion, s32[]{:T(128)S(6)} %select_n.168, ...), kind=kOutput, calls=%fused_computation.12 | convolution fusion | flops 1612447744 | bytes 11534340 | tf_op jit(solution)/shard_map/dot_general | solution.py:79
  108.2 1.6 copy.44
  109.8 3.7 %all-to-all-start.1 = ((f32[4,16,8,8,128]{4,1,2,3,0:T(8,128)}), f32[4,16,8,8,128]{4,1,2,3,0:T(8,128)S(1)}, u32[]{:S(2)}, u32[]{:S(2)}) async-start(f32[4,16,8,8,128]{4,1,2,3,0:T(8,128)} %copy.44), calls=%async_computation.1 | async-start | bytes 4194304 | tf_op jit(solution)/shard_map/all_to_all | solution.py:86
  114.9 1.3 multiply_add_fusion
  116.3 1.3 broadcast_xor_fusion.1
  118.1 20.4 %all-to-all-done.1 = f32[4,16,8,8,128]{4,1,2,3,0:T(8,128)S(1)} async-done(((f32[4,16,8,8,128]{4,1,2,3,0:T(8,128)}), f32[4,16,8,8,128]{4,1,2,3,0:T(8,128)S(1)}, u32[]{:S(2)}, u32[]{:S(2)}) %all-to-all-start.1) | async-done | bytes 2097184 | tf_op jit(solution)/shard_map/all_to_all | solution.py:86
  138.7 1.0 copy.46
  139.7 6.5 %all-to-all-start.2 = ((f32[16,8,8,128]{3,1,2,0:T(8,128)}), f32[16,8,8,128]{3,1,2,0:T(8,128)S(1)}, u32[]{:S(2)}, u32[]{:S(2)}) async-start(f32[16,8,8,128]{3,1,2,0:T(8,128)} %copy.46), calls=%async_computation.2 | async-start | bytes 1048576 | tf_op jit(solution)/shard_map/all_to_all | solution.py:87
  147.4 15.9 %all-to-all-done.2 = f32[16,8,8,128]{3,1,2,0:T(8,128)S(1)} async-done(((f32[16,8,8,128]{3,1,2,0:T(8,128)}), f32[16,8,8,128]{3,1,2,0:T(8,128)S(1)}, u32[]{:S(2)}, u32[]{:S(2)}) %all-to-all-start.2) | async-done | bytes 524320 | tf_op jit(solution)/shard_map/all_to_all | solution.py:87
  (47 shorter events, 6.8 us)
Async XLA Ops:
  8.3 6.0 %copy-start.1 = (f32[2,8,128,128]{3,2,1,0:T(8,128)S(1)}, f32[2,8,128,128]{3,2,1,0:T(8,128)}, u32[]{:S(2)}) copy-start(f32[2,8,128,128]{3,2,1,0:T(8,128)} %param.7) | copy-start | bytes 3145732
  11.0 75.0 %collective-permute-start = (f32[8,128,2,512]{3,1,2,0:T(8,128)}, f32[8,128,2,512]{3,1,2,0:T(8,128)}, u32[]{:S(2)}, u32[]{:S(2)}) collective-permute-start(f32[8,128,2,512]{3,1,2,0:T(8,128)} %bitcast.71), channel_id=1, source_target_pairs={{0,4},{4,0},{1,5},{5,1},{2,6},{6,2},{3,7},{7,3},{8,12},{12,8},{9,1... | collective-permute-start | bytes 12582920 | tf_op jit(solution)/shard_map/ppermute | solution.py:46
  14.5 42.6 %copy-start.3 = (s32[8]{0:T(128)S(1)}, s32[8]{0:T(128)}, u32[]{:S(2)}) copy-start(s32[8]{0:T(128)} %param.10) | copy-start | bytes 100
  14.5 43.1 %copy-start.4 = (s32[8]{0:T(128)S(1)}, s32[8]{0:T(128)}, u32[]{:S(2)}) copy-start(s32[8]{0:T(128)} %param.9) | copy-start | bytes 100
  54.4 26.2 %collective-permute-start.1 = (f32[64,4,8,128]{3,0,1,2:T(8,128)}, f32[64,4,8,128]{3,0,1,2:T(8,128)S(1)}, u32[]{:S(2)}, u32[]{:S(2)}) collective-permute-start(f32[64,4,8,128]{3,0,1,2:T(8,128)} %copy.39), channel_id=1, source_target_pairs={{0,1},{1,2},{2,3},{3,0},{4,5},{5,6},{6,7},{7,4},{8,9},{9,10},{10,1... | collective-permute-start | bytes 3145736 | tf_op jit(solution)/shard_map/ppermute | solution.py:46
  55.6 25.9 %collective-permute-start.2 = (f32[64,4,8,128]{3,0,1,2:T(8,128)}, f32[64,4,8,128]{3,0,1,2:T(8,128)}, u32[]{:S(2)}, u32[]{:S(2)}) collective-permute-start(f32[64,4,8,128]{3,0,1,2:T(8,128)} %copy.39), channel_id=1, source_target_pairs={{0,3},{1,0},{2,1},{3,2},{4,7},{5,4},{6,5},{7,6},{8,11},{9,8},{10,9... | collective-permute-start | bytes 3145736 | tf_op jit(solution)/shard_map/ppermute | solution.py:46
  80.5 5.5 %copy-start = (f32[64,4,8,128]{3,0,1,2:T(8,128)}, f32[64,4,8,128]{3,0,1,2:T(8,128)S(1)}, u32[]{:S(2)}) copy-start(f32[64,4,8,128]{3,0,1,2:T(8,128)S(1)} %collective-permute-done.1) | copy-start | bytes 3145732
  81.4 23.5 %collective-permute-start.3 = (f32[32,4,8,128]{3,0,1,2:T(8,128)}, f32[32,4,8,128]{3,0,1,2:T(8,128)S(1)}, u32[]{:S(2)}, u32[]{:S(2)}) collective-permute-start(f32[32,4,8,128]{3,0,1,2:T(8,128)} %slice.36), channel_id=1, source_target_pairs={{0,1},{1,2},{2,3},{3,0},{4,5},{5,6},{6,7},{7,4},{8,9},{9,10},{10,1... | collective-permute-start | bytes 1572872 | tf_op jit(solution)/shard_map/ppermute | solution.py:46
  83.4 21.5 %collective-permute-start.4 = (f32[32,4,8,128]{3,0,1,2:T(8,128)}, f32[32,4,8,128]{3,0,1,2:T(8,128)}, u32[]{:S(2)}, u32[]{:S(2)}) collective-permute-start(f32[32,4,8,128]{3,0,1,2:T(8,128)} %slice.37), channel_id=1, source_target_pairs={{0,3},{1,0},{2,1},{3,2},{4,7},{5,4},{6,5},{7,6},{8,11},{9,8},{10,9... | collective-permute-start | bytes 1572872 | tf_op jit(solution)/shard_map/ppermute | solution.py:46
  109.8 8.0 %copy-start.5 = (f32[64]{0:T(128)S(1)}, f32[64]{0:T(128)}, u32[]{:S(2)}) copy-start(f32[64]{0:T(128)} %param.12) | copy-start | bytes 772
  109.8 28.7 %all-to-all-start.1 = ((f32[4,16,8,8,128]{4,1,2,3,0:T(8,128)}), f32[4,16,8,8,128]{4,1,2,3,0:T(8,128)S(1)}, u32[]{:S(2)}, u32[]{:S(2)}) async-start(f32[4,16,8,8,128]{4,1,2,3,0:T(8,128)} %copy.44), calls=%async_computation.1 | async-start | bytes 4194304 | tf_op jit(solution)/shard_map/all_to_all | solution.py:86
  118.1 28.0 %copy-start.2 = (f32[512]{0:T(512)S(1)}, f32[512]{0:T(512)}, u32[]{:S(2)}) copy-start(f32[512]{0:T(512)} %param.13) | copy-start | bytes 6148
  139.7 23.7 %all-to-all-start.2 = ((f32[16,8,8,128]{3,1,2,0:T(8,128)}), f32[16,8,8,128]{3,1,2,0:T(8,128)S(1)}, u32[]{:S(2)}, u32[]{:S(2)}) async-start(f32[16,8,8,128]{3,1,2,0:T(8,128)} %copy.46), calls=%async_computation.2 | async-start | bytes 1048576 | tf_op jit(solution)/shard_map/all_to_all | solution.py:87
